TPU v7x, 512 devices: a whole 4x8x8 slice. The times are simulated.
512 devices in a mesh: orb: 32 (over z, y_lo, core), dom: 16 (over x, y_hi).
Axes of the slice: x: 4, y: 8 (y_hi: 4, y_lo: 2; y = y_hi * 2 + y_lo), z: 8, core: 2. Of those that a mesh axis runs over, the one named last changes fastest.
Arguments:
- orbitals: bfloat16 [32, 16, 192, 128], P('orb', None, 'dom'), may hold values from -6 to 6
- potential: float32 [16, 192, 128], P(None, 'dom'), may hold values from 0 to 2
- degree: int32 [32], P('orb'), may hold values from 1 to 8, as said below
- owners: int32 [4], replicated, may hold values from 0 to 31
- rotation: bfloat16 [4, 1, 32], P(None, None, 'orb'), may hold values from -3 to 3
Outputs:
- filtered: float32 [32, 16, 192, 128], P('orb', None, 'dom')
- rotated: float32 [32, 16, 192, 128], P('orb', None, 'dom')
Inputs may be any that keep to these rules, and one draw needn't show every extreme that they name: Every draw has an orbital of degree 8 and one of degree 1. `owners`: panel numbers; panel q holds orbital q alone.
All inputs are finite; a program needn't handle non-finite values.
Results may differ from a plain program's by a relative error of at most 0.0003.
Values sent between devices are 32-bit elements; how exact they have to be, the bound alone decides.
A program may use at most 64 MiB of HBM per device.

v0:
```python
import jax
import jax.numpy as jnp
from jax import lax
from jax.sharding import PartitionSpec as P

RADIUS = 6
MAXDEG = 8
STEPS = 4
STENCIL = (
    -5369.0 / 1800.0,
    12.0 / 7.0,
    -15.0 / 56.0,
    10.0 / 189.0,
    -1.0 / 112.0,
    2.0 / 1925.0,
    -1.0 / 16632.0,
)
FILTER_CENTER = 7.75
FILTER_HALF = 6.25


def padded_2(block, sides, width):
    for axis, dim in sides:
        count = lax.axis_size(axis)
        forward = [(i, i + 1) for i in range(count - 1)]
        backward = [(target, source) for source, target in forward]
        low = lax.ppermute(
            lax.slice_in_dim(block, block.shape[dim] - width, None, axis=dim), axis, forward
        )
        high = lax.ppermute(lax.slice_in_dim(block, 0, width, axis=dim), axis, backward)
        block = jnp.concatenate([low, block, high], axis=dim)
    return block


def from_root(shard, axis, root):
    mine = lax.axis_index(axis) == root
    return lax.psum(jnp.where(mine, shard, jnp.zeros_like(shard)), axis)


def apply_hamiltonian(padded, potential):
    width = padded.shape[2] - 2 * RADIUS
    center = padded[:, :, RADIUS : RADIUS + width]
    laplace = 3.0 * STENCIL[0] * center
    for offset in range(1, RADIUS + 1):
        beside = (
            padded[:, :, RADIUS + offset : RADIUS + offset + width]
            + padded[:, :, RADIUS - offset : RADIUS - offset + width]
        )
        beside = beside + jnp.roll(center, offset, 3) + jnp.roll(center, -offset, 3)
        beside = beside + jnp.roll(center, offset, 1) + jnp.roll(center, -offset, 1)
        laplace = laplace + STENCIL[offset] * beside
    return -0.5 * laplace + potential * center


def chebyshev_next(applied, current, previous, first):
    shifted = applied - FILTER_CENTER * current
    if first:
        return shifted / FILTER_HALF
    return 2.0 / FILTER_HALF * shifted - previous


def keep_degree(selected, advanced, degree, level):
    return jnp.where((degree == level)[:, None, None, None], advanced, selected)


def per_device(orbitals, potential, degree, owners, rotation):
    block_rows = orbitals.shape[0]
    current = orbitals.astype(jnp.float32)
    previous = current
    selected = jnp.zeros_like(current)
    for section in range(MAXDEG):
        padded = padded_2(current, (("dom", 2),), RADIUS)
        applied = apply_hamiltonian(padded, potential)
        advanced = chebyshev_next(applied, current, previous, section == 0)
        selected = keep_degree(selected, advanced, degree, section + 1)
        previous, current = (current, advanced)
    flattened = selected.reshape(block_rows, -1)
    rotated = jnp.zeros(flattened.shape, jnp.float32)
    for section in range(STEPS):
        panel_block = from_root(flattened, "orb", owners[section])
        coefficients = rotation[section].astype(jnp.float32)
        rotated = rotated + lax.dot_general(
            coefficients,
            panel_block,
            (((0,), (0,)), ((), ())),
            precision=lax.Precision.HIGHEST,
            preferred_element_type=jnp.float32,
        )
    rotated = rotated.reshape(selected.shape)
    return (selected, rotated)


def solution(mesh):
    placed = (
        P("orb", None, "dom", None),
        P(None, "dom", None),
        P("orb"),
        P(),
        P(None, None, "orb"),
    )
    return jax.shard_map(
        per_device,
        mesh=mesh,
        in_specs=placed,
        out_specs=(P("orb", None, "dom", None), P("orb", None, "dom", None)),
        check_vma=False,
    )
```

profile of v0, /device:TPU:1, one launch (start us, length us, event | category | flops | bytes accessed | tf_op | source)
XLA Modules:
  0.0 363.2 jit_solution(5902551951845159628)
XLA Ops:
  7.2 1.4 fusion.652
  8.7 1.3 collective-permute-start
  10.0 6.3 %collective-permute-start.1 = (f32[1,16,6,128]{3,1,2,0:T(8,128)}, f32[1,16,6,128]{3,1,2,0:T(8,128)}, u32[]{:S(2)}, u32[]{:S(2)}) collective-permute-start(f32[1,16,6,128]{3,1,2,0:T(8,128)} %get-tuple-element.406), channel_id=1, source_target_pairs={{0,1},{1,2},{2,3},{3,4},{4,5},{5,6},{6,7},{7,8},{8,9},{9,10},{10,1... | collective-permute-start | bytes 147464 | tf_op jit(solution)/shard_map/ppermute | solution.py:27
  27.2 1.8 broadcast_multiply_fusion
  30.4 1.3 collective-permute-start.2
  31.7 5.5 %collective-permute-start.3 = (f32[1,16,6,128]{3,1,2,0:T(8,128)S(1)}, f32[1,16,6,128]{3,1,2,0:T(8,128)S(1)}, u32[]{:S(2)}, u32[]{:S(2)}) collective-permute-start(f32[1,16,6,128]{3,1,2,0:T(8,128)S(1)} %get-tuple-element.364), channel_id=1, source_target_pairs={{0,1},{1,2},{2,3},{3,4},{4,5},{5,6},{6,7},{7,8},{8,9},{9,10},{10,1... | collective-permute-start | bytes 147464 | tf_op jit(solution)/shard_map/ppermute | solution.py:27
  37.2 1.1 collective-permute-done.3
  40.4 1.3 collective-permute-start.4
  41.7 6.1 %collective-permute-start.5 = (f32[1,16,6,128]{3,1,2,0:T(8,128)S(1)}, f32[1,16,6,128]{3,1,2,0:T(8,128)S(1)}, u32[]{:S(2)}, u32[]{:S(2)}) collective-permute-start(f32[1,16,6,128]{3,1,2,0:T(8,128)S(1)} %get-tuple-element.314), channel_id=1, source_target_pairs={{0,1},{1,2},{2,3},{3,4},{4,5},{5,6},{6,7},{7,8},{8,9},{9,10},{10,1... | collective-permute-start | bytes 147464 | tf_op jit(solution)/shard_map/ppermute | solution.py:27
  47.8 1.1 collective-permute-done.5
  51.0 1.3 collective-permute-start.6
  52.3 6.9 %collective-permute-start.7 = (f32[1,16,6,128]{3,1,2,0:T(8,128)S(1)}, f32[1,16,6,128]{3,1,2,0:T(8,128)S(1)}, u32[]{:S(2)}, u32[]{:S(2)}) collective-permute-start(f32[1,16,6,128]{3,1,2,0:T(8,128)S(1)} %get-tuple-element.264), channel_id=1, source_target_pairs={{0,1},{1,2},{2,3},{3,4},{4,5},{5,6},{6,7},{7,8},{8,9},{9,10},{10,1... | collective-permute-start | bytes 147464 | tf_op jit(solution)/shard_map/ppermute | solution.py:27
  59.2 1.1 collective-permute-done.7
  62.4 1.3 collective-permute-start.8
  63.7 6.5 %collective-permute-start.9 = (f32[1,16,6,128]{3,1,2,0:T(8,128)S(1)}, f32[1,16,6,128]{3,1,2,0:T(8,128)S(1)}, u32[]{:S(2)}, u32[]{:S(2)}) collective-permute-start(f32[1,16,6,128]{3,1,2,0:T(8,128)S(1)} %get-tuple-element.214), channel_id=1, source_target_pairs={{0,1},{1,2},{2,3},{3,4},{4,5},{5,6},{6,7},{7,8},{8,9},{9,10},{10,1... | collective-permute-start | bytes 147464 | tf_op jit(solution)/shard_map/ppermute | solution.py:27
  70.2 1.1 collective-permute-done.9
  73.4 1.3 collective-permute-start.10
  74.7 6.4 %collective-permute-start.11 = (f32[1,16,6,128]{3,1,2,0:T(8,128)S(1)}, f32[1,16,6,128]{3,1,2,0:T(8,128)S(1)}, u32[]{:S(2)}, u32[]{:S(2)}) collective-permute-start(f32[1,16,6,128]{3,1,2,0:T(8,128)S(1)} %get-tuple-element.164), channel_id=1, source_target_pairs={{0,1},{1,2},{2,3},{3,4},{4,5},{5,6},{6,7},{7,8},{8,9},{9,10},{10,1... | collective-permute-start | bytes 147464 | tf_op jit(solution)/shard_map/ppermute | solution.py:27
  81.1 1.1 collective-permute-done.11
  84.3 1.3 collective-permute-start.12
  85.6 6.4 %collective-permute-start.13 = (f32[1,16,6,128]{3,1,2,0:T(8,128)S(1)}, f32[1,16,6,128]{3,1,2,0:T(8,128)S(1)}, u32[]{:S(2)}, u32[]{:S(2)}) collective-permute-start(f32[1,16,6,128]{3,1,2,0:T(8,128)S(1)} %get-tuple-element.114), channel_id=1, source_target_pairs={{0,1},{1,2},{2,3},{3,4},{4,5},{5,6},{6,7},{7,8},{8,9},{9,10},{10,1... | collective-permute-start | bytes 147464 | tf_op jit(solution)/shard_map/ppermute | solution.py:27
  92.0 1.1 collective-permute-done.13
  95.2 1.3 collective-permute-start.14
  96.5 6.7 %collective-permute-start.15 = (f32[1,16,6,128]{3,1,2,0:T(8,128)S(1)}, f32[1,16,6,128]{3,1,2,0:T(8,128)S(1)}, u32[]{:S(2)}, u32[]{:S(2)}) collective-permute-start(f32[1,16,6,128]{3,1,2,0:T(8,128)S(1)} %get-tuple-element.56), channel_id=1, source_target_pairs={{0,1},{1,2},{2,3},{3,4},{4,5},{5,6},{6,7},{7,8},{8,9},{9,10},{10,1... | collective-permute-start | bytes 147464 | tf_op jit(solution)/shard_map/ppermute | solution.py:27
  103.3 1.5 collective-permute-done.15
  104.8 0.7 broadcast_select_fusion.3
  106.2 0.7 select_n.108
  106.9 0.7 select_n.111
  107.7 0.7 select_n.114
  108.5 0.7 select_n.105
  112.4 241.8 %all-reduce.3.cloned.1.call-done = (f32[1,24576]{1,0:T(1,128)}, f32[1,24576]{1,0:T(1,128)}, f32[1,24576]{1,0:T(1,128)}, f32[1,24576]{1,0:T(1,128)}) async-done(((f32[1,24576]{1,0:T(1,128)}, f32[1,24576]{1,0:T(1,128)}, f32[1,24576]{1,0:T(1,128)}, f32[1,24576]{1,0:T(1,128)}), (f32[1,24576]{1,0:T(1,128)}, f32[1,24576]{1,0:T(1,128)}, f32[1,24576]{1,0:T(1,128)}, ...) | async-done | bytes 393232 | tf_op jit(solution)/shard_map/psum | solution.py:37
  354.2 1.4 add_reduce_fusion
  (242 shorter events, 22.2 us)
Async XLA Ops:
  7.2 347.0 %all-reduce.3.cloned.1.call-start = ((), (), s32[]{:S(2)}) async-start(), calls=%async_computation | async-start | bytes 786432 | tf_op jit(solution)/shard_map/psum | solution.py:37
  7.2 9.0 %copy-start = (bf16[1,16,12,128]{3,1,2,0:T(8,128)(2,1)S(1)}, bf16[1,16,12,128]{3,1,2,0:T(8,128)(2,1)}, u32[]{:S(2)}) copy-start(bf16[1,16,12,128]{3,1,2,0:T(8,128)(2,1)} %param.5) | copy-start | bytes 147460
  8.7 17.8 %collective-permute-start = (f32[1,16,6,128]{3,1,2,0:T(8,128)}, f32[1,16,6,128]{3,1,2,0:T(8,128)}, u32[]{:S(2)}, u32[]{:S(2)}) collective-permute-start(f32[1,16,6,128]{3,1,2,0:T(8,128)} %get-tuple-element.405), channel_id=1, source_target_pairs={{1,0},{2,1},{3,2},{4,3},{5,4},{6,5},{7,6},{8,7},{9,8},{10,9},{11,1... | collective-permute-start | bytes 147464 | tf_op jit(solution)/shard_map/ppermute | solution.py:30
  10.0 16.5 %collective-permute-start.1 = (f32[1,16,6,128]{3,1,2,0:T(8,128)}, f32[1,16,6,128]{3,1,2,0:T(8,128)}, u32[]{:S(2)}, u32[]{:S(2)}) collective-permute-start(f32[1,16,6,128]{3,1,2,0:T(8,128)} %get-tuple-element.406), channel_id=1, source_target_pairs={{0,1},{1,2},{2,3},{3,4},{4,5},{5,6},{6,7},{7,8},{8,9},{9,10},{10,1... | collective-permute-start | bytes 147464 | tf_op jit(solution)/shard_map/ppermute | solution.py:27
  20.6 1.8 copy-start.6
  23.2 3.3 copy-start.1
  26.5 0.7 copy-start.3
  26.5 0.7 copy-start.4
  26.5 0.7 copy-start.5
  30.4 6.8 %collective-permute-start.2 = (f32[1,16,6,128]{3,1,2,0:T(8,128)S(1)}, f32[1,16,6,128]{3,1,2,0:T(8,128)S(1)}, u32[]{:S(2)}, u32[]{:S(2)}) collective-permute-start(f32[1,16,6,128]{3,1,2,0:T(8,128)S(1)} %get-tuple-element.363), channel_id=1, source_target_pairs={{1,0},{2,1},{3,2},{4,3},{5,4},{6,5},{7,6},{8,7},{9,8},{10,9},{11,1... | collective-permute-start | bytes 147464 | tf_op jit(solution)/shard_map/ppermute | solution.py:30
  31.7 6.7 %collective-permute-start.3 = (f32[1,16,6,128]{3,1,2,0:T(8,128)S(1)}, f32[1,16,6,128]{3,1,2,0:T(8,128)S(1)}, u32[]{:S(2)}, u32[]{:S(2)}) collective-permute-start(f32[1,16,6,128]{3,1,2,0:T(8,128)S(1)} %get-tuple-element.364), channel_id=1, source_target_pairs={{0,1},{1,2},{2,3},{3,4},{4,5},{5,6},{6,7},{7,8},{8,9},{9,10},{10,1... | collective-permute-start | bytes 147464 | tf_op jit(solution)/shard_map/ppermute | solution.py:27
  40.4 7.4 %collective-permute-start.4 = (f32[1,16,6,128]{3,1,2,0:T(8,128)S(1)}, f32[1,16,6,128]{3,1,2,0:T(8,128)S(1)}, u32[]{:S(2)}, u32[]{:S(2)}) collective-permute-start(f32[1,16,6,128]{3,1,2,0:T(8,128)S(1)} %get-tuple-element.313), channel_id=1, source_target_pairs={{1,0},{2,1},{3,2},{4,3},{5,4},{6,5},{7,6},{8,7},{9,8},{10,9},{11,1... | collective-permute-start | bytes 147464 | tf_op jit(solution)/shard_map/ppermute | solution.py:30
  41.7 7.3 %collective-permute-start.5 = (f32[1,16,6,128]{3,1,2,0:T(8,128)S(1)}, f32[1,16,6,128]{3,1,2,0:T(8,128)S(1)}, u32[]{:S(2)}, u32[]{:S(2)}) collective-permute-start(f32[1,16,6,128]{3,1,2,0:T(8,128)S(1)} %get-tuple-element.314), channel_id=1, source_target_pairs={{0,1},{1,2},{2,3},{3,4},{4,5},{5,6},{6,7},{7,8},{8,9},{9,10},{10,1... | collective-permute-start | bytes 147464 | tf_op jit(solution)/shard_map/ppermute | solution.py:27
  51.0 8.3 %collective-permute-start.6 = (f32[1,16,6,128]{3,1,2,0:T(8,128)S(1)}, f32[1,16,6,128]{3,1,2,0:T(8,128)S(1)}, u32[]{:S(2)}, u32[]{:S(2)}) collective-permute-start(f32[1,16,6,128]{3,1,2,0:T(8,128)S(1)} %get-tuple-element.263), channel_id=1, source_target_pairs={{1,0},{2,1},{3,2},{4,3},{5,4},{6,5},{7,6},{8,7},{9,8},{10,9},{11,1... | collective-permute-start | bytes 147464 | tf_op jit(solution)/shard_map/ppermute | solution.py:30
  52.3 8.1 %collective-permute-start.7 = (f32[1,16,6,128]{3,1,2,0:T(8,128)S(1)}, f32[1,16,6,128]{3,1,2,0:T(8,128)S(1)}, u32[]{:S(2)}, u32[]{:S(2)}) collective-permute-start(f32[1,16,6,128]{3,1,2,0:T(8,128)S(1)} %get-tuple-element.264), channel_id=1, source_target_pairs={{0,1},{1,2},{2,3},{3,4},{4,5},{5,6},{6,7},{7,8},{8,9},{9,10},{10,1... | collective-permute-start | bytes 147464 | tf_op jit(solution)/shard_map/ppermute | solution.py:27
  62.4 7.8 %collective-permute-start.8 = (f32[1,16,6,128]{3,1,2,0:T(8,128)S(1)}, f32[1,16,6,128]{3,1,2,0:T(8,128)S(1)}, u32[]{:S(2)}, u32[]{:S(2)}) collective-permute-start(f32[1,16,6,128]{3,1,2,0:T(8,128)S(1)} %get-tuple-element.213), channel_id=1, source_target_pairs={{1,0},{2,1},{3,2},{4,3},{5,4},{6,5},{7,6},{8,7},{9,8},{10,9},{11,1... | collective-permute-start | bytes 147464 | tf_op jit(solution)/shard_map/ppermute | solution.py:30
  63.7 7.6 %collective-permute-start.9 = (f32[1,16,6,128]{3,1,2,0:T(8,128)S(1)}, f32[1,16,6,128]{3,1,2,0:T(8,128)S(1)}, u32[]{:S(2)}, u32[]{:S(2)}) collective-permute-start(f32[1,16,6,128]{3,1,2,0:T(8,128)S(1)} %get-tuple-element.214), channel_id=1, source_target_pairs={{0,1},{1,2},{2,3},{3,4},{4,5},{5,6},{6,7},{7,8},{8,9},{9,10},{10,1... | collective-permute-start | bytes 147464 | tf_op jit(solution)/shard_map/ppermute | solution.py:27
  73.4 7.7 %collective-permute-start.10 = (f32[1,16,6,128]{3,1,2,0:T(8,128)S(1)}, f32[1,16,6,128]{3,1,2,0:T(8,128)S(1)}, u32[]{:S(2)}, u32[]{:S(2)}) collective-permute-start(f32[1,16,6,128]{3,1,2,0:T(8,128)S(1)} %get-tuple-element.163), channel_id=1, source_target_pairs={{1,0},{2,1},{3,2},{4,3},{5,4},{6,5},{7,6},{8,7},{9,8},{10,9},{11,1... | collective-permute-start | bytes 147464 | tf_op jit(solution)/shard_map/ppermute | solution.py:30
  74.7 7.6 %collective-permute-start.11 = (f32[1,16,6,128]{3,1,2,0:T(8,128)S(1)}, f32[1,16,6,128]{3,1,2,0:T(8,128)S(1)}, u32[]{:S(2)}, u32[]{:S(2)}) collective-permute-start(f32[1,16,6,128]{3,1,2,0:T(8,128)S(1)} %get-tuple-element.164), channel_id=1, source_target_pairs={{0,1},{1,2},{2,3},{3,4},{4,5},{5,6},{6,7},{7,8},{8,9},{9,10},{10,1... | collective-permute-start | bytes 147464 | tf_op jit(solution)/shard_map/ppermute | solution.py:27
  84.3 7.7 %collective-permute-start.12 = (f32[1,16,6,128]{3,1,2,0:T(8,128)S(1)}, f32[1,16,6,128]{3,1,2,0:T(8,128)S(1)}, u32[]{:S(2)}, u32[]{:S(2)}) collective-permute-start(f32[1,16,6,128]{3,1,2,0:T(8,128)S(1)} %get-tuple-element.113), channel_id=1, source_target_pairs={{1,0},{2,1},{3,2},{4,3},{5,4},{6,5},{7,6},{8,7},{9,8},{10,9},{11,1... | collective-permute-start | bytes 147464 | tf_op jit(solution)/shard_map/ppermute | solution.py:30
  85.6 7.6 %collective-permute-start.13 = (f32[1,16,6,128]{3,1,2,0:T(8,128)S(1)}, f32[1,16,6,128]{3,1,2,0:T(8,128)S(1)}, u32[]{:S(2)}, u32[]{:S(2)}) collective-permute-start(f32[1,16,6,128]{3,1,2,0:T(8,128)S(1)} %get-tuple-element.114), channel_id=1, source_target_pairs={{0,1},{1,2},{2,3},{3,4},{4,5},{5,6},{6,7},{7,8},{8,9},{9,10},{10,1... | collective-permute-start | bytes 147464 | tf_op jit(solution)/shard_map/ppermute | solution.py:27
  95.2 8.1 %collective-permute-start.14 = (f32[1,16,6,128]{3,1,2,0:T(8,128)S(1)}, f32[1,16,6,128]{3,1,2,0:T(8,128)S(1)}, u32[]{:S(2)}, u32[]{:S(2)}) collective-permute-start(f32[1,16,6,128]{3,1,2,0:T(8,128)S(1)} %get-tuple-element.55), channel_id=1, source_target_pairs={{1,0},{2,1},{3,2},{4,3},{5,4},{6,5},{7,6},{8,7},{9,8},{10,9},{11,1... | collective-permute-start | bytes 147464 | tf_op jit(solution)/shard_map/ppermute | solution.py:30
  96.5 8.2 %collective-permute-start.15 = (f32[1,16,6,128]{3,1,2,0:T(8,128)S(1)}, f32[1,16,6,128]{3,1,2,0:T(8,128)S(1)}, u32[]{:S(2)}, u32[]{:S(2)}) collective-permute-start(f32[1,16,6,128]{3,1,2,0:T(8,128)S(1)} %get-tuple-element.56), channel_id=1, source_target_pairs={{0,1},{1,2},{2,3},{3,4},{4,5},{5,6},{6,7},{7,8},{8,9},{9,10},{10,1... | collective-permute-start | bytes 147464 | tf_op jit(solution)/shard_map/ppermute | solution.py:27
  105.5 0.6 copy-start.2
  107.7 1.5 copy-start.7
Sparse Core Ops, SparseCore 0:
  109.4 244.7 all-reduce.2
where the time goes:
time: 364 us; the launch traced here: 363 us
  waiting for transfers between devices  250 us (69%)
  starting transfers between devices  61.2 us (17%)
  local copies, waits for them, and re-layouts  22.4 us (6%)
  between operations  21.5 us (6%)
  other arithmetic  8.01 us (2%)
    psum x1, waiting for transfers between devices, from_root(): return lax.psum(jnp.where(mine, shard, jnp.zeros_like(shard)), axis)  242 us
    ppermute x8, starting transfers between devices, padded_2(): lax.ppermute(lax.slice_in_dim(block, block.shape[dim] - width, None, axis...  50.8 us
    ppermute x8, starting transfers between devices, padded_2(): lax.ppermute(lax.slice_in_dim(block, 0, width, axis=dim), axis, backward)  10.3 us
    slice x96, local copies, waits for them, and re-layouts, apply_hamiltonian(): beside = beside + jnp.roll(center, offset, 3) + jnp.roll(center, -offset, 3)  8.87 us
    ppermute x8, waiting for transfers between devices, padded_2(): lax.ppermute(lax.slice_in_dim(block, block.shape[dim] - width, None, axis...  8.25 us
  transfers between devices with their start and end apart: 17, of which 8 were waited for; matrix products, arithmetic and copies ran while one was open for 2% of the time, Pallas kernels for 0%

commit v1 on v0

--- a/solution.py
+++ b/solution.py
@@ -19,6 +19,12 @@
 FILTER_HALF = 6.25
 
 
+def add_all(x, axis):
+    parts = lax.all_gather(x, axis, axis=0, tiled=False)
+    result = parts.sum(axis=0)
+    return result
+
+
 def padded_2(block, sides, width):
     for axis, dim in sides:
         count = lax.axis_size(axis)
@@ -34,7 +40,7 @@
 
 def from_root(shard, axis, root):
     mine = lax.axis_index(axis) == root
-    return lax.psum(jnp.where(mine, shard, jnp.zeros_like(shard)), axis)
+    return add_all(jnp.where(mine, shard, jnp.zeros_like(shard)), axis)
 
 
 def apply_hamiltonian(padded, potential):

time: 364 us -> 432 us (1.19)
  waiting for transfers between devices: 250 us -> 297 us
  other arithmetic: 8.01 us -> 22.5 us
  local copies, waits for them, and re-layouts: 22.4 us -> 28.1 us
    all_gather x0 -> x4, waiting for transfers between devices: none -> 289 us  [add_all(): parts = lax.all_gather(x, axis, axis=0, tiled=False)]
    psum x1 -> x0, waiting for transfers between devices: 242 us -> none  [from_root(): return lax.psum(jnp.where(mine, shard, jnp.zeros_like(shard)), axis)]
    reduce_sum x0 -> x4, other arithmetic: none -> 15.7 us  [add_all(): result = parts.sum(axis=0)]
    slice x96, local copies, waits for them, and re-layouts: 8.87 us -> 14.1 us  [apply_hamiltonian(): beside = beside + jnp.roll(center, offset, 3) + jnp.roll(center, -offset, 3)]
  transfers between devices with their start and end apart: 17 -> 20, of which waited for: 8 -> 11; matrix products, arithmetic and copies ran while one was open for 2% -> 7% of each run, Pallas kernels for 0% -> 0%
where the time goes in v1:
time: 432 us; the launch traced here: 431 us
  waiting for transfers between devices  297 us (69%)
  starting transfers between devices  61.5 us (14%)
  local copies, waits for them, and re-layouts  28.1 us (7%)
  other arithmetic  22.5 us (5%)
  between operations  21.2 us (5%)
    all_gather x4, waiting for transfers between devices, add_all(): parts = lax.all_gather(x, axis, axis=0, tiled=False)  289 us
    ppermute x8, starting transfers between devices, padded_2(): lax.ppermute(lax.slice_in_dim(block, block.shape[dim] - width, None, axis...  51 us
    reduce_sum x4, other arithmetic, add_all(): result = parts.sum(axis=0)  15.7 us
    slice x96, local copies, waits for them, and re-layouts, apply_hamiltonian(): beside = beside + jnp.roll(center, offset, 3) + jnp.roll(center, -offset, 3)  14.1 us
    ppermute x8, starting transfers between devices, padded_2(): lax.ppermute(lax.slice_in_dim(block, 0, width, axis=dim), axis, backward)  10.3 us
  transfers between devices with their start and end apart: 20, of which 11 were waited for; matrix products, arithmetic and copies ran while one was open for 7% of the time, Pallas kernels for 0%

profile of v1, /device:TPU:1, one launch (start us, length us, event | category | flops | bytes accessed | tf_op | source)
XLA Modules:
  0.0 430.8 jit_solution(2391849489792869376)
XLA Ops:
  7.2 1.4 fusion.652
  8.6 1.3 collective-permute-start
  9.9 6.3 %collective-permute-start.1 = (f32[1,16,6,128]{3,1,2,0:T(8,128)}, f32[1,16,6,128]{3,1,2,0:T(8,128)}, u32[]{:S(2)}, u32[]{:S(2)}) collective-permute-start(f32[1,16,6,128]{3,1,2,0:T(8,128)} %get-tuple-element.404), channel_id=1, source_target_pairs={{0,1},{1,2},{2,3},{3,4},{4,5},{5,6},{6,7},{7,8},{8,9},{9,10},{10,1... | collective-permute-start | bytes 147464 | tf_op jit(solution)/shard_map/ppermute | solution.py:33
  33.4 1.9 broadcast_multiply_fusion
  36.7 1.3 collective-permute-start.2
  38.0 5.5 %collective-permute-start.3 = (f32[1,16,6,128]{3,1,2,0:T(8,128)S(1)}, f32[1,16,6,128]{3,1,2,0:T(8,128)S(1)}, u32[]{:S(2)}, u32[]{:S(2)}) collective-permute-start(f32[1,16,6,128]{3,1,2,0:T(8,128)S(1)} %get-tuple-element.362), channel_id=1, source_target_pairs={{0,1},{1,2},{2,3},{3,4},{4,5},{5,6},{6,7},{7,8},{8,9},{9,10},{10,1... | collective-permute-start | bytes 147464 | tf_op jit(solution)/shard_map/ppermute | solution.py:33
  43.5 1.1 collective-permute-done.3
  46.7 1.3 collective-permute-start.4
  48.0 6.1 %collective-permute-start.5 = (f32[1,16,6,128]{3,1,2,0:T(8,128)S(1)}, f32[1,16,6,128]{3,1,2,0:T(8,128)S(1)}, u32[]{:S(2)}, u32[]{:S(2)}) collective-permute-start(f32[1,16,6,128]{3,1,2,0:T(8,128)S(1)} %get-tuple-element.312), channel_id=1, source_target_pairs={{0,1},{1,2},{2,3},{3,4},{4,5},{5,6},{6,7},{7,8},{8,9},{9,10},{10,1... | collective-permute-start | bytes 147464 | tf_op jit(solution)/shard_map/ppermute | solution.py:33
  54.1 1.1 collective-permute-done.5
  57.3 1.3 collective-permute-start.6
  58.6 6.9 %collective-permute-start.7 = (f32[1,16,6,128]{3,1,2,0:T(8,128)S(1)}, f32[1,16,6,128]{3,1,2,0:T(8,128)S(1)}, u32[]{:S(2)}, u32[]{:S(2)}) collective-permute-start(f32[1,16,6,128]{3,1,2,0:T(8,128)S(1)} %get-tuple-element.262), channel_id=1, source_target_pairs={{0,1},{1,2},{2,3},{3,4},{4,5},{5,6},{6,7},{7,8},{8,9},{9,10},{10,1... | collective-permute-start | bytes 147464 | tf_op jit(solution)/shard_map/ppermute | solution.py:33
  65.6 1.1 collective-permute-done.7
  68.8 1.3 collective-permute-start.8
  70.1 6.5 %collective-permute-start.9 = (f32[1,16,6,128]{3,1,2,0:T(8,128)S(1)}, f32[1,16,6,128]{3,1,2,0:T(8,128)S(1)}, u32[]{:S(2)}, u32[]{:S(2)}) collective-permute-start(f32[1,16,6,128]{3,1,2,0:T(8,128)S(1)} %get-tuple-element.212), channel_id=1, source_target_pairs={{0,1},{1,2},{2,3},{3,4},{4,5},{5,6},{6,7},{7,8},{8,9},{9,10},{10,1... | collective-permute-start | bytes 147464 | tf_op jit(solution)/shard_map/ppermute | solution.py:33
  76.6 1.1 collective-permute-done.9
  79.7 1.3 collective-permute-start.10
  81.0 6.4 %collective-permute-start.11 = (f32[1,16,6,128]{3,1,2,0:T(8,128)S(1)}, f32[1,16,6,128]{3,1,2,0:T(8,128)S(1)}, u32[]{:S(2)}, u32[]{:S(2)}) collective-permute-start(f32[1,16,6,128]{3,1,2,0:T(8,128)S(1)} %get-tuple-element.162), channel_id=1, source_target_pairs={{0,1},{1,2},{2,3},{3,4},{4,5},{5,6},{6,7},{7,8},{8,9},{9,10},{10,1... | collective-permute-start | bytes 147464 | tf_op jit(solution)/shard_map/ppermute | solution.py:33
  87.5 1.1 collective-permute-done.11
  90.7 1.3 collective-permute-start.12
  92.0 6.4 %collective-permute-start.13 = (f32[1,16,6,128]{3,1,2,0:T(8,128)S(1)}, f32[1,16,6,128]{3,1,2,0:T(8,128)S(1)}, u32[]{:S(2)}, u32[]{:S(2)}) collective-permute-start(f32[1,16,6,128]{3,1,2,0:T(8,128)S(1)} %get-tuple-element.112), channel_id=1, source_target_pairs={{0,1},{1,2},{2,3},{3,4},{4,5},{5,6},{6,7},{7,8},{8,9},{9,10},{10,1... | collective-permute-start | bytes 147464 | tf_op jit(solution)/shard_map/ppermute | solution.py:33
  101.6 1.3 collective-permute-start.14
  102.9 6.9 %collective-permute-start.15 = (f32[1,16,6,128]{3,1,2,0:T(8,128)S(1)}, f32[1,16,6,128]{3,1,2,0:T(8,128)S(1)}, u32[]{:S(2)}, u32[]{:S(2)}) collective-permute-start(f32[1,16,6,128]{3,1,2,0:T(8,128)S(1)} %get-tuple-element.54), channel_id=1, source_target_pairs={{0,1},{1,2},{2,3},{3,4},{4,5},{5,6},{6,7},{7,8},{8,9},{9,10},{10,1... | collective-permute-start | bytes 147464 | tf_op jit(solution)/shard_map/ppermute | solution.py:33
  109.8 1.3 collective-permute-done.15
  118.4 89.0 %all-gather.7.cloned.1.call-done = f32[32,1,24576]{2,1,0:T(1,128)} async-done(((f32[1,1,24576]{2,1,0:T(1,128)}), f32[32,1,24576]{2,1,0:T(1,128)}) %all-gather.7.cloned.1.call-update) | async-done | bytes 3145744 | tf_op jit(solution)/shard_map/all_gather | solution.py:23
  207.5 3.9 reduce_sum.37
  211.4 66.6 %all-gather.9.cloned.1.call-done = f32[32,1,24576]{2,1,0:T(1,128)} async-done(((f32[1,1,24576]{2,1,0:T(1,128)}), f32[32,1,24576]{2,1,0:T(1,128)}) %all-gather.9.cloned.1.call-update) | async-done | bytes 3145744 | tf_op jit(solution)/shard_map/all_gather | solution.py:23
  278.0 3.9 reduce_sum.38
  282.0 67.2 %all-gather.11.cloned.1.call-done = f32[32,1,24576]{2,1,0:T(1,128)} async-done(((f32[1,1,24576]{2,1,0:T(1,128)}), f32[32,1,24576]{2,1,0:T(1,128)}) %all-gather.11.cloned.1.call-update) | async-done | bytes 3145744 | tf_op jit(solution)/shard_map/all_gather | solution.py:23
  349.2 3.9 reduce_sum.39
  353.1 66.5 %all-gather.5.cloned.1.call-done = f32[32,1,24576]{2,1,0:T(1,128)} async-done(((f32[1,1,24576]{2,1,0:T(1,128)}), f32[32,1,24576]{2,1,0:T(1,128)}) %all-gather.5.cloned.1.call-update) | async-done | bytes 3145744 | tf_op jit(solution)/shard_map/all_gather | solution.py:23
  419.6 3.9 reduce_sum.36
  (249 shorter events, 33.0 us)
Async XLA Ops:
  7.2 16.6 %copy-start = (bf16[1,16,12,128]{3,1,2,0:T(8,128)(2,1)S(1)}, bf16[1,16,12,128]{3,1,2,0:T(8,128)(2,1)}, u32[]{:S(2)}) copy-start(bf16[1,16,12,128]{3,1,2,0:T(8,128)(2,1)} %param.5) | copy-start | bytes 147460
  7.2 200.3 %all-gather.7.cloned.1.call-start = ((), (), s32[]{:S(2)}) async-start(), calls=%async_computation.1 | async-start | bytes 3244032 | tf_op jit(solution)/shard_map/all_gather | solution.py:23
  8.6 24.8 %collective-permute-start = (f32[1,16,6,128]{3,1,2,0:T(8,128)}, f32[1,16,6,128]{3,1,2,0:T(8,128)}, u32[]{:S(2)}, u32[]{:S(2)}) collective-permute-start(f32[1,16,6,128]{3,1,2,0:T(8,128)} %get-tuple-element.403), channel_id=1, source_target_pairs={{1,0},{2,1},{3,2},{4,3},{5,4},{6,5},{7,6},{8,7},{9,8},{10,9},{11,1... | collective-permute-start | bytes 147464 | tf_op jit(solution)/shard_map/ppermute | solution.py:36
  9.9 23.5 %collective-permute-start.1 = (f32[1,16,6,128]{3,1,2,0:T(8,128)}, f32[1,16,6,128]{3,1,2,0:T(8,128)}, u32[]{:S(2)}, u32[]{:S(2)}) collective-permute-start(f32[1,16,6,128]{3,1,2,0:T(8,128)} %get-tuple-element.404), channel_id=1, source_target_pairs={{0,1},{1,2},{2,3},{3,4},{4,5},{5,6},{6,7},{7,8},{8,9},{9,10},{10,1... | collective-permute-start | bytes 147464 | tf_op jit(solution)/shard_map/ppermute | solution.py:33
  20.0 9.5 %copy-start.3 = (s32[4]{0:T(128)S(1)}, s32[4]{0:T(128)}, u32[]{:S(2)}) copy-start(s32[4]{0:T(128)} %param.8) | copy-start | bytes 52
  20.0 13.4 %copy-start.1 = (f32[16,12,128]{2,0,1:T(8,128)S(1)}, f32[16,12,128]{2,0,1:T(8,128)}, u32[]{:S(2)}) copy-start(f32[16,12,128]{2,0,1:T(8,128)} %param.6) | copy-start | bytes 294916
  36.7 6.8 %collective-permute-start.2 = (f32[1,16,6,128]{3,1,2,0:T(8,128)S(1)}, f32[1,16,6,128]{3,1,2,0:T(8,128)S(1)}, u32[]{:S(2)}, u32[]{:S(2)}) collective-permute-start(f32[1,16,6,128]{3,1,2,0:T(8,128)S(1)} %get-tuple-element.361), channel_id=1, source_target_pairs={{1,0},{2,1},{3,2},{4,3},{5,4},{6,5},{7,6},{8,7},{9,8},{10,9},{11,1... | collective-permute-start | bytes 147464 | tf_op jit(solution)/shard_map/ppermute | solution.py:36
  38.0 6.7 %collective-permute-start.3 = (f32[1,16,6,128]{3,1,2,0:T(8,128)S(1)}, f32[1,16,6,128]{3,1,2,0:T(8,128)S(1)}, u32[]{:S(2)}, u32[]{:S(2)}) collective-permute-start(f32[1,16,6,128]{3,1,2,0:T(8,128)S(1)} %get-tuple-element.362), channel_id=1, source_target_pairs={{0,1},{1,2},{2,3},{3,4},{4,5},{5,6},{6,7},{7,8},{8,9},{9,10},{10,1... | collective-permute-start | bytes 147464 | tf_op jit(solution)/shard_map/ppermute | solution.py:33
  46.7 7.4 %collective-permute-start.4 = (f32[1,16,6,128]{3,1,2,0:T(8,128)S(1)}, f32[1,16,6,128]{3,1,2,0:T(8,128)S(1)}, u32[]{:S(2)}, u32[]{:S(2)}) collective-permute-start(f32[1,16,6,128]{3,1,2,0:T(8,128)S(1)} %get-tuple-element.311), channel_id=1, source_target_pairs={{1,0},{2,1},{3,2},{4,3},{5,4},{6,5},{7,6},{8,7},{9,8},{10,9},{11,1... | collective-permute-start | bytes 147464 | tf_op jit(solution)/shard_map/ppermute | solution.py:36
  48.0 7.3 %collective-permute-start.5 = (f32[1,16,6,128]{3,1,2,0:T(8,128)S(1)}, f32[1,16,6,128]{3,1,2,0:T(8,128)S(1)}, u32[]{:S(2)}, u32[]{:S(2)}) collective-permute-start(f32[1,16,6,128]{3,1,2,0:T(8,128)S(1)} %get-tuple-element.312), channel_id=1, source_target_pairs={{0,1},{1,2},{2,3},{3,4},{4,5},{5,6},{6,7},{7,8},{8,9},{9,10},{10,1... | collective-permute-start | bytes 147464 | tf_op jit(solution)/shard_map/ppermute | solution.py:33
  57.3 8.3 %collective-permute-start.6 = (f32[1,16,6,128]{3,1,2,0:T(8,128)S(1)}, f32[1,16,6,128]{3,1,2,0:T(8,128)S(1)}, u32[]{:S(2)}, u32[]{:S(2)}) collective-permute-start(f32[1,16,6,128]{3,1,2,0:T(8,128)S(1)} %get-tuple-element.261), channel_id=1, source_target_pairs={{1,0},{2,1},{3,2},{4,3},{5,4},{6,5},{7,6},{8,7},{9,8},{10,9},{11,1... | collective-permute-start | bytes 147464 | tf_op jit(solution)/shard_map/ppermute | solution.py:36
  58.6 8.1 %collective-permute-start.7 = (f32[1,16,6,128]{3,1,2,0:T(8,128)S(1)}, f32[1,16,6,128]{3,1,2,0:T(8,128)S(1)}, u32[]{:S(2)}, u32[]{:S(2)}) collective-permute-start(f32[1,16,6,128]{3,1,2,0:T(8,128)S(1)} %get-tuple-element.262), channel_id=1, source_target_pairs={{0,1},{1,2},{2,3},{3,4},{4,5},{5,6},{6,7},{7,8},{8,9},{9,10},{10,1... | collective-permute-start | bytes 147464 | tf_op jit(solution)/shard_map/ppermute | solution.py:33
  68.8 7.8 %collective-permute-start.8 = (f32[1,16,6,128]{3,1,2,0:T(8,128)S(1)}, f32[1,16,6,128]{3,1,2,0:T(8,128)S(1)}, u32[]{:S(2)}, u32[]{:S(2)}) collective-permute-start(f32[1,16,6,128]{3,1,2,0:T(8,128)S(1)} %get-tuple-element.211), channel_id=1, source_target_pairs={{1,0},{2,1},{3,2},{4,3},{5,4},{6,5},{7,6},{8,7},{9,8},{10,9},{11,1... | collective-permute-start | bytes 147464 | tf_op jit(solution)/shard_map/ppermute | solution.py:36
  70.1 7.6 %collective-permute-start.9 = (f32[1,16,6,128]{3,1,2,0:T(8,128)S(1)}, f32[1,16,6,128]{3,1,2,0:T(8,128)S(1)}, u32[]{:S(2)}, u32[]{:S(2)}) collective-permute-start(f32[1,16,6,128]{3,1,2,0:T(8,128)S(1)} %get-tuple-element.212), channel_id=1, source_target_pairs={{0,1},{1,2},{2,3},{3,4},{4,5},{5,6},{6,7},{7,8},{8,9},{9,10},{10,1... | collective-permute-start | bytes 147464 | tf_op jit(solution)/shard_map/ppermute | solution.py:33
  79.7 7.7 %collective-permute-start.10 = (f32[1,16,6,128]{3,1,2,0:T(8,128)S(1)}, f32[1,16,6,128]{3,1,2,0:T(8,128)S(1)}, u32[]{:S(2)}, u32[]{:S(2)}) collective-permute-start(f32[1,16,6,128]{3,1,2,0:T(8,128)S(1)} %get-tuple-element.161), channel_id=1, source_target_pairs={{1,0},{2,1},{3,2},{4,3},{5,4},{6,5},{7,6},{8,7},{9,8},{10,9},{11,1... | collective-permute-start | bytes 147464 | tf_op jit(solution)/shard_map/ppermute | solution.py:36
  81.0 7.6 %collective-permute-start.11 = (f32[1,16,6,128]{3,1,2,0:T(8,128)S(1)}, f32[1,16,6,128]{3,1,2,0:T(8,128)S(1)}, u32[]{:S(2)}, u32[]{:S(2)}) collective-permute-start(f32[1,16,6,128]{3,1,2,0:T(8,128)S(1)} %get-tuple-element.162), channel_id=1, source_target_pairs={{0,1},{1,2},{2,3},{3,4},{4,5},{5,6},{6,7},{7,8},{8,9},{9,10},{10,1... | collective-permute-start | bytes 147464 | tf_op jit(solution)/shard_map/ppermute | solution.py:33
  90.7 7.7 %collective-permute-start.12 = (f32[1,16,6,128]{3,1,2,0:T(8,128)S(1)}, f32[1,16,6,128]{3,1,2,0:T(8,128)S(1)}, u32[]{:S(2)}, u32[]{:S(2)}) collective-permute-start(f32[1,16,6,128]{3,1,2,0:T(8,128)S(1)} %get-tuple-element.111), channel_id=1, source_target_pairs={{1,0},{2,1},{3,2},{4,3},{5,4},{6,5},{7,6},{8,7},{9,8},{10,9},{11,1... | collective-permute-start | bytes 147464 | tf_op jit(solution)/shard_map/ppermute | solution.py:36
  92.0 7.6 %collective-permute-start.13 = (f32[1,16,6,128]{3,1,2,0:T(8,128)S(1)}, f32[1,16,6,128]{3,1,2,0:T(8,128)S(1)}, u32[]{:S(2)}, u32[]{:S(2)}) collective-permute-start(f32[1,16,6,128]{3,1,2,0:T(8,128)S(1)} %get-tuple-element.112), channel_id=1, source_target_pairs={{0,1},{1,2},{2,3},{3,4},{4,5},{5,6},{6,7},{7,8},{8,9},{9,10},{10,1... | collective-permute-start | bytes 147464 | tf_op jit(solution)/shard_map/ppermute | solution.py:33
  101.6 8.2 %collective-permute-start.14 = (f32[1,16,6,128]{3,1,2,0:T(8,128)S(1)}, f32[1,16,6,128]{3,1,2,0:T(8,128)S(1)}, u32[]{:S(2)}, u32[]{:S(2)}) collective-permute-start(f32[1,16,6,128]{3,1,2,0:T(8,128)S(1)} %get-tuple-element.53), channel_id=1, source_target_pairs={{1,0},{2,1},{3,2},{4,3},{5,4},{6,5},{7,6},{8,7},{9,8},{10,9},{11,1... | collective-permute-start | bytes 147464 | tf_op jit(solution)/shard_map/ppermute | solution.py:36
  102.9 8.2 %collective-permute-start.15 = (f32[1,16,6,128]{3,1,2,0:T(8,128)S(1)}, f32[1,16,6,128]{3,1,2,0:T(8,128)S(1)}, u32[]{:S(2)}, u32[]{:S(2)}) collective-permute-start(f32[1,16,6,128]{3,1,2,0:T(8,128)S(1)} %get-tuple-element.54), channel_id=1, source_target_pairs={{0,1},{1,2},{2,3},{3,4},{4,5},{5,6},{6,7},{7,8},{8,9},{9,10},{10,1... | collective-permute-start | bytes 147464 | tf_op jit(solution)/shard_map/ppermute | solution.py:33
  111.1 4.2 copy-start.4
  111.8 170.1 %copy-start.2 = (f32[1,16,12,128]{3,1,2,0:T(8,128)}, f32[1,16,12,128]{3,1,2,0:T(8,128)S(1)}, u32[]{:S(2)}) copy-start(f32[1,16,12,128]{3,1,2,0:T(8,128)S(1)} %get-tuple-element.7) | copy-start | bytes 294916
  112.7 165.3 %all-gather.9.cloned.1.call-start = ((), (), s32[]{:S(2)}) async-start(), calls=%async_computation.2 | async-start | bytes 3244032 | tf_op jit(solution)/shard_map/all_gather | solution.py:23
  113.5 235.6 %all-gather.11.cloned.1.call-start = ((), (), s32[]{:S(2)}) async-start(), calls=%async_computation.3 | async-start | bytes 3244032 | tf_op jit(solution)/shard_map/all_gather | solution.py:23
  114.4 305.2 %all-gather.5.cloned.1.call-start = ((), (), s32[]{:S(2)}) async-start(), calls=%async_computation | async-start | bytes 3244032 | tf_op jit(solution)/shard_map/all_gather | solution.py:23
Sparse Core Ops, SparseCore 0:
  112.8 94.6 all-gather.6
  209.6 68.3 all-gather.8
  280.8 68.3 all-gather.10
  351.2 68.3 all-gather.4
